TPU v7x, 256 devices: a whole 4x4x8 slice. The times are simulated.
256 devices in a mesh: seq: 32 (over z, x), head: 8 (over y, core).
Axes of the slice: x: 4, y: 4, z: 8, core: 2. Of those that a mesh axis runs over, the one named last changes fastest.
Arguments:
- queries: bfloat16 [16384, 1024], P(('seq', 'head')), may hold values from -24 to 24
- keys: bfloat16 [16384, 1024], P(('seq', 'head')), may hold values from -6 to 6
- values: bfloat16 [16384, 1024], P(('seq', 'head')), may hold values from -6 to 6
- out_grad: bfloat16 [16384, 1024], P(('seq', 'head')), may hold values from -6 to 6
- key_blocks: int32 [128, 8], replicated, may hold values from 0 to 127, as said below
- counts: int32 [128], replicated, may hold values from 2 to 8, as said below
Outputs:
- attention: bfloat16 [16384, 1024], P('seq', 'head')
- query_grad: bfloat16 [16384, 1024], P('seq', 'head')
- key_grad: bfloat16 [16384, 1024], P('seq', 'head')
- value_grad: bfloat16 [16384, 1024], P('seq', 'head')
Inputs may be any that keep to these rules, and one draw needn't show every extreme that they name: `counts`: some query block uses all 8 listed blocks. `key_blocks`: row a lists 8 different blocks, the first being block a itself and the second block (a - 1) modulo 128; only the first counts[a] of them are used.
All inputs are finite; a program needn't handle non-finite values.
Results may differ from a plain program's by a relative error of at most 0.015.
Values may be sent and summed in bfloat16 or wider, within the bound.
A program may use at most 64 MiB of HBM per device.

v0:
```python
import math
import jax
import jax.numpy as jnp
from jax import lax
from jax.sharding import PartitionSpec as P

HEADS = 8
BLK = 128
neg_fill = -1e30
tile_limit = 512


def block_table(key_blocks, counts):
    block_count = key_blocks.shape[0]
    slot_ids = jnp.arange(key_blocks.shape[1])
    live_slot = slot_ids[None, :] < counts[:, None]
    matches = (key_blocks[:, :, None] == jnp.arange(block_count)[None, None, :]) & live_slot[
        :, :, None
    ]
    return jnp.any(matches, axis=1).astype(jnp.float32)


def one_hot_rows(first_row, row_total, block_count):
    block_ids = (first_row + jnp.arange(row_total)) // BLK
    return (block_ids[:, None] == jnp.arange(block_count)[None, :]).astype(jnp.float32)


def on_device(queries, keys, values, out_grad, key_blocks, counts):
    heads_here = HEADS // lax.axis_size("head")
    q_rows, k_rows, v_rows, g_rows = (
        lax.all_to_all(queries, "head", split_axis=1, concat_axis=0, tiled=True),
        lax.all_to_all(keys, "head", split_axis=1, concat_axis=0, tiled=True),
        lax.all_to_all(values, "head", split_axis=1, concat_axis=0, tiled=True),
        lax.all_to_all(out_grad, "head", split_axis=1, concat_axis=0, tiled=True),
    )
    row_count = q_rows.shape[0]
    feat_width = q_rows.shape[1]
    head_dim = feat_width // heads_here
    score_scale = 1.0 / math.sqrt(head_dim)
    block_count = key_blocks.shape[0]
    slot_total = key_blocks.shape[1]
    local_blocks = row_count // BLK
    first_block = lax.axis_index("seq") * local_blocks
    listed = lax.dynamic_slice_in_dim(key_blocks, first_block, local_blocks, 0)
    used = lax.dynamic_slice_in_dim(counts, first_block, local_blocks, 0)
    slot_ids = jnp.arange(slot_total)
    live = jnp.repeat(slot_ids[None, :] < used[:, None], BLK, axis=1)
    live_mask = live[:, None, None, :]

    def listed_sets(k_whole, v_whole):
        k_blocks = k_whole.reshape(block_count, BLK, heads_here, head_dim)
        v_blocks = v_whole.reshape(block_count, BLK, heads_here, head_dim)
        key_set = jnp.take(k_blocks, listed, axis=0).reshape(
            local_blocks, slot_total * BLK, heads_here, head_dim
        )
        value_set = jnp.take(v_blocks, listed, axis=0).reshape(
            local_blocks, slot_total * BLK, heads_here, head_dim
        )
        return (key_set, value_set)

    q_blocks = q_rows.reshape(local_blocks, BLK, heads_here, head_dim)
    g_blocks = g_rows.reshape(local_blocks, BLK, heads_here, head_dim)

    def block_scores(key_set):
        scores = (
            jnp.einsum("bqhd,bkhd->bhqk", q_blocks, key_set, preferred_element_type=jnp.float32)
            * score_scale
        )
        return jnp.where(live_mask, scores, neg_fill)

    k_whole, v_whole = (
        lax.all_gather(k_rows, "seq", axis=0, tiled=True),
        lax.all_gather(v_rows, "seq", axis=0, tiled=True),
    )
    key_set, value_set = listed_sets(k_whole, v_whole)
    scores = block_scores(key_set)
    row_max = jnp.max(scores, axis=3)
    weights = jnp.where(live_mask, jnp.exp(scores - row_max[..., None]), 0.0)
    row_sum = jnp.sum(weights, axis=3)
    mixed = jnp.einsum(
        "bhqk,bkhd->bqhd",
        weights.astype(jnp.bfloat16),
        value_set,
        preferred_element_type=jnp.float32,
    )
    attention = (mixed / jnp.transpose(row_sum, (0, 2, 1))[..., None]).astype(jnp.bfloat16)
    block_total = row_max + jnp.log(row_sum)
    block_dot = jnp.sum(g_blocks.astype(jnp.float32) * attention.astype(jnp.float32), axis=3)
    dot_bhq = jnp.transpose(block_dot, (0, 2, 1))
    log_total = jnp.transpose(block_total, (0, 2, 1)).reshape(row_count, heads_here)
    grad_dot = block_dot.reshape(row_count, heads_here)
    k_second, v_second = (
        lax.all_gather(k_rows, "seq", axis=0, tiled=True),
        lax.all_gather(v_rows, "seq", axis=0, tiled=True),
    )
    key_again, value_again = listed_sets(k_second, v_second)
    scores_again = block_scores(key_again)
    probs = jnp.where(live_mask, jnp.exp(scores_again - block_total[..., None]), 0.0)
    dprob = jnp.einsum("bqhd,bkhd->bhqk", g_blocks, value_again, preferred_element_type=jnp.float32)
    dscore = (probs * (dprob - dot_bhq[..., None])).astype(jnp.bfloat16)
    query_acc = jnp.einsum("bhqk,bkhd->bqhd", dscore, key_again, preferred_element_type=jnp.float32)
    all_log_total, all_grad_dot = (
        lax.all_gather(log_total, "seq", axis=0, tiled=True),
        lax.all_gather(grad_dot, "seq", axis=0, tiled=True),
    )
    table = block_table(key_blocks, counts)
    local_hot = one_hot_rows(lax.axis_index("seq") * row_count, row_count, block_count)
    key_table = jnp.einsum("bc,kc->bk", table, local_hot)
    k_heads = k_rows.reshape(row_count, heads_here, head_dim)
    v_heads = v_rows.reshape(row_count, heads_here, head_dim)
    zero_heads = jnp.zeros((row_count, heads_here, head_dim), jnp.float32)
    q_piece = lax.all_gather(q_rows, "seq", axis=0, tiled=True)
    g_piece = lax.all_gather(g_rows, "seq", axis=0, tiled=True)
    piece_rows = q_piece.shape[0]
    tile_rows = math.gcd(piece_rows, tile_limit)

    def tile(tile_index, fold_state):
        offset = tile_index * tile_rows
        q_tile = lax.dynamic_slice_in_dim(q_piece, offset, tile_rows, 0).reshape(
            tile_rows, heads_here, head_dim
        )
        g_tile = lax.dynamic_slice_in_dim(g_piece, offset, tile_rows, 0).reshape(
            tile_rows, heads_here, head_dim
        )
        total_tile = lax.dynamic_slice_in_dim(all_log_total, offset, tile_rows, 0)
        dot_tile = lax.dynamic_slice_in_dim(all_grad_dot, offset, tile_rows, 0)
        query_hot = one_hot_rows(offset, tile_rows, block_count)
        allowed = jnp.einsum("qb,bk->qk", query_hot, key_table) > 0.5
        tile_scores = (
            jnp.einsum("qhd,khd->qhk", q_tile, k_heads, preferred_element_type=jnp.float32)
            * score_scale
        )
        tile_scores = jnp.where(allowed[:, None, :], tile_scores, neg_fill)
        tile_probs = jnp.where(
            allowed[:, None, :], jnp.exp(tile_scores - total_tile[:, :, None]), 0.0
        )
        value_acc = fold_state[1] + jnp.einsum(
            "qhk,qhd->khd",
            tile_probs.astype(jnp.bfloat16),
            g_tile,
            preferred_element_type=jnp.float32,
        )
        tile_dprob = jnp.einsum("qhd,khd->qhk", g_tile, v_heads, preferred_element_type=jnp.float32)
        tile_ds = (tile_probs * (tile_dprob - dot_tile[:, :, None])).astype(jnp.bfloat16)
        key_acc = fold_state[0] + jnp.einsum(
            "qhk,qhd->khd", tile_ds, q_tile, preferred_element_type=jnp.float32
        )
        return (key_acc, value_acc)

    key_acc, value_acc = lax.fori_loop(0, piece_rows // tile_rows, tile, (zero_heads, zero_heads))
    query_grad = (query_acc * score_scale).astype(jnp.bfloat16).reshape(row_count, feat_width)
    key_grad = (key_acc * score_scale).astype(jnp.bfloat16).reshape(row_count, feat_width)
    value_grad = value_acc.astype(jnp.bfloat16).reshape(row_count, feat_width)
    return (attention.reshape(row_count, feat_width), query_grad, key_grad, value_grad)


def solution(mesh):
    in_specs = (
        P(("seq", "head"), None),
        P(("seq", "head"), None),
        P(("seq", "head"), None),
        P(("seq", "head"), None),
        P(),
        P(),
    )
    out_specs = (P("seq", "head"), P("seq", "head"), P("seq", "head"), P("seq", "head"))
    return jax.shard_map(
        on_device, mesh=mesh, in_specs=in_specs, out_specs=out_specs, check_vma=False
    )
```

profile of v0, /device:TPU:8, one launch (start us, length us, event | category | flops | bytes accessed | tf_op | source)
XLA Modules:
  0.0 496.2 jit_solution(53246647357267488)
XLA Ops:
  8.1 9.9 %all_to_all.76 = bf16[64,8,128]{2,0,1:T(8,128)(2,1)} all-to-all(bf16[64,8,128]{2,0,1:T(8,128)(2,1)S(1)} %copy_bitcast_fusion.2), channel_id=1, replica_groups=mesh['seq'=32,'head'=8] {'head'}, dimensions={1} | all-to-all | bytes 262144 | tf_op jit(solution)/shard_map/all_to_all | solution.py:32
  19.0 9.2 %all_to_all.77 = bf16[64,8,128]{2,0,1:T(8,128)(2,1)} all-to-all(bf16[64,8,128]{2,0,1:T(8,128)(2,1)S(1)} %copy_bitcast_fusion.3), channel_id=1, replica_groups=mesh['seq'=32,'head'=8] {'head'}, dimensions={1} | all-to-all | bytes 262144 | tf_op jit(solution)/shard_map/all_to_all | solution.py:33
  29.1 9.2 %all_to_all.78 = bf16[64,8,128]{2,0,1:T(8,128)(2,1)} all-to-all(bf16[64,8,128]{2,0,1:T(8,128)(2,1)S(1)} %copy_bitcast_fusion.1), channel_id=1, replica_groups=mesh['seq'=32,'head'=8] {'head'}, dimensions={1} | all-to-all | bytes 262144 | tf_op jit(solution)/shard_map/all_to_all | solution.py:31
  39.3 9.2 %all_to_all.79 = bf16[64,8,128]{2,0,1:T(8,128)(2,1)} all-to-all(bf16[64,8,128]{2,0,1:T(8,128)(2,1)S(1)} %copy_bitcast_fusion), channel_id=1, replica_groups=mesh['seq'=32,'head'=8] {'head'}, dimensions={1} | all-to-all | bytes 262144 | tf_op jit(solution)/shard_map/all_to_all | solution.py:34
  50.0 51.3 %all-gather.7.cloned.1.call-done = bf16[16384,128]{1,0:T(8,128)(2,1)} async-done(((bf16[512,128]{1,0:T(8,128)(2,1)}), bf16[16384,128]{1,0:T(8,128)(2,1)}) %all-gather.7.cloned.1.call-update) | async-done | bytes 4194320 | tf_op jit(solution)/shard_map/all_gather | solution.py:72
  101.3 2.9 gather_fusion.1
  104.3 78.2 %all-gather.5.cloned.1.call-done = bf16[16384,128]{1,0:T(8,128)(2,1)} async-done(((bf16[512,128]{1,0:T(8,128)(2,1)}), bf16[16384,128]{1,0:T(8,128)(2,1)}) %all-gather.5.cloned.1.call-update) | async-done | bytes 4194320 | tf_op jit(solution)/shard_map/all_gather | solution.py:73
  182.5 2.9 gather_fusion
  188.5 47.6 %all_gather.23 = f32[16384,1]{0,1:T(1,128)S(1)} all-gather(f32[512,1]{0,1:T(1,128)S(1)} %bitcast.245), channel_id=1, replica_groups=mesh['seq'=32,'head'=8] {'seq'}, dimensions={0}, use_global_device_ids=true | all-gather | bytes 67584 | tf_op jit(solution)/shard_map/all_gather | solution.py:103
  236.1 2.7 fusion.54
  238.8 47.4 %all_gather.25 = f32[16384,1]{0,1:T(1,128)S(1)} all-gather(f32[512,1]{0,1:T(1,128)S(1)} %bitcast.246), channel_id=1, replica_groups=mesh['seq'=32,'head'=8] {'seq'}, dimensions={0}, use_global_device_ids=true | all-gather | bytes 67584 | tf_op jit(solution)/shard_map/all_gather | solution.py:104
  286.1 3.5 fusion.41
  289.6 55.2 %all-gather.11.cloned.1.call-done = bf16[16384,128]{1,0:T(8,128)(2,1)} async-done(((bf16[512,128]{1,0:T(8,128)(2,1)}), bf16[16384,128]{1,0:T(8,128)(2,1)}) %all-gather.11.cloned.1.call-update) | async-done | bytes 4194320 | tf_op jit(solution)/shard_map/all_gather | solution.py:113
  344.8 143.3 %while.18 = (s32[]{:T(128)}, f32[512,1,128]{0,2,1:T(8,128)S(1)}, f32[512,1,128]{0,2,1:T(8,128)S(1)}, bf16[16384,128]{1,0:T(8,128)(2,1)}, bf16[128,512]{1,0:T(8,1...) while((s32[]{:T(128)}, f32[512,1,128]{0,2,1:T(8,128)S(1)}, ...), condition=%wide.region_5.7_spmd.clone, body=%wide.region_4.6_spmd.clone.sunk | while | flops 338239488 | bytes 5654229 | solution.py:150
  345.2 1.4 fusion.96
  346.6 1.5 fusion.97
  349.7 1.4 fusion.96
  351.1 1.5 fusion.97
  354.2 1.4 fusion.96
  355.5 1.5 fusion.97
  358.6 1.4 fusion.96
  360.0 1.5 fusion.97
  363.1 1.4 fusion.96
  364.5 1.5 fusion.97
  367.6 1.4 fusion.96
  369.0 1.5 fusion.97
  372.1 1.4 fusion.96
  373.5 1.5 fusion.97
  376.6 1.4 fusion.96
  377.9 1.5 fusion.97
  381.0 1.4 fusion.96
  382.4 1.5 fusion.97
  385.5 1.4 fusion.96
  386.9 1.5 fusion.97
  390.0 1.4 fusion.96
  391.4 1.5 fusion.97
  395.8 1.5 fusion.97
  400.3 1.5 fusion.97
  403.4 1.4 fusion.96
  404.8 1.5 fusion.97
  409.3 1.5 fusion.97
  413.7 1.5 fusion.97
  416.8 1.4 fusion.96
  418.2 1.5 fusion.97
  422.7 1.5 fusion.97
  427.2 1.5 fusion.97
  430.3 1.4 fusion.96
  431.7 1.5 fusion.97
  436.1 1.5 fusion.97
  440.6 1.5 fusion.97
  443.7 1.4 fusion.96
  445.1 1.5 fusion.97
  449.6 1.5 fusion.97
  454.0 1.5 fusion.97
  457.1 1.4 fusion.96
  458.5 1.5 fusion.97
  463.0 1.5 fusion.97
  467.5 1.5 fusion.97
  470.6 1.4 fusion.96
  472.0 1.5 fusion.97
  476.4 1.5 fusion.97
  480.9 1.5 fusion.97
  484.0 1.4 fusion.96
  485.4 1.5 fusion.97
  (196 shorter events, 78.6 us)
Async XLA Ops:
  7.2 0.9 copy-start
  7.2 41.3 %copy-start.7 = (s32[128,8]{0,1:T(8,128)S(1)}, s32[128,8]{0,1:T(8,128)}, u32[]{:S(2)}) copy-start(s32[128,8]{0,1:T(8,128)} %param.14) | copy-start | bytes 12292
  7.2 41.8 %copy-start.8 = (s32[128]{0:T(128)S(1)}, s32[128]{0:T(128)}, u32[]{:S(2)}) copy-start(s32[128]{0:T(128)} %param.15) | copy-start | bytes 1540
  7.2 94.1 %all-gather.7.cloned.1.call-start = ((), (), s32[]{:S(2)}) async-start(), calls=%async_computation.5 | async-start | bytes 4325376 | tf_op jit(solution)/shard_map/all_gather | solution.py:72
  18.0 164.5 %all-gather.5.cloned.1.call-start = ((), (), s32[]{:S(2)}) async-start(), calls=%async_computation.4 | async-start | bytes 4325376 | tf_op jit(solution)/shard_map/all_gather | solution.py:73
  28.2 261.5 %all-gather.9.cloned.1.call-start = ((), (), s32[]{:S(2)}) async-start(), calls=%async_computation.6 | async-start | bytes 4325376 | tf_op jit(solution)/shard_map/all_gather | solution.py:112
  38.3 306.5 %all-gather.11.cloned.1.call-start = ((), (), s32[]{:S(2)}) async-start(), calls=%async_computation.7 | async-start | bytes 4325376 | tf_op jit(solution)/shard_map/all_gather | solution.py:113
  185.4 0.9 copy-start.5
  185.7 2.7 copy-start.2
  185.7 50.3 %copy-start.3 = (bf16[4,8,128,1,128]{4,2,1,0,3:T(8,128)(2,1)}, bf16[4,8,128,1,128]{4,2,1,0,3:T(8,128)(2,1)S(1)}, u32[]{:S(2)}) copy-start(bf16[4,8,128,1,128]{4,2,1,0,3:T(8,128)(2,1)S(1)} %get-tuple-element.309) | copy-start | bytes 3145732
  186.3 49.7 %copy-start.6 = (bf16[64,8,128]{2,0,1:T(8,128)(2,1)S(1)}, bf16[64,8,128]{2,0,1:T(8,128)(2,1)}, u32[]{:S(2)}) copy-start(bf16[64,8,128]{2,0,1:T(8,128)(2,1)} %all_to_all.79) | copy-start | bytes 393220
  286.1 58.7 %copy-start.1 = (bf16[64,8,128]{2,0,1:T(8,128)(2,1)S(1)}, bf16[64,8,128]{2,0,1:T(8,128)(2,1)}, u32[]{:S(2)}) copy-start(bf16[64,8,128]{2,0,1:T(8,128)(2,1)} %all_to_all.77) | copy-start | bytes 393220
  286.1 58.7 %copy-start.4 = (bf16[64,8,128]{2,0,1:T(8,128)(2,1)S(1)}, bf16[64,8,128]{2,0,1:T(8,128)(2,1)}, u32[]{:S(2)}) copy-start(bf16[64,8,128]{2,0,1:T(8,128)(2,1)} %all_to_all.76) | copy-start | bytes 393220
Sparse Core Ops, SparseCore 0:
  18.1 83.1 all-gather.6
  103.9 78.5 all-gather.4
  185.1 78.5 all-gather.8
  266.1 78.6 all-gather.10
where the time goes:
time: 498 us; the launch traced here: 496 us
  waiting for transfers between devices  185 us (37%)
  matrix products  148 us (30%)
  blocking collectives  132 us (27%)
  between operations  14 us (3%)
  local copies, waits for them, and re-layouts  11.9 us (2%)
    all_gather x1, waiting for transfers between devices, on_device(): lax.all_gather(v_rows, 'seq', axis=0, tiled=True)  78.2 us
    all_gather x1, waiting for transfers between devices, on_device(): g_piece = lax.all_gather(g_rows, 'seq', axis=0, tiled=True)  55.2 us
    all_gather x1, waiting for transfers between devices, on_device(): lax.all_gather(k_rows, 'seq', axis=0, tiled=True)  51.3 us
    dot_general x32, matrix products, tile(): jnp.einsum('qhk,qhd->khd', tile_ds, q_tile, preferred_element_type=jnp.fl...  47.7 us
    all_gather x1, blocking collectives, on_device(): lax.all_gather(log_total, 'seq', axis=0, tiled=True)  47.6 us
    all_gather x1, blocking collectives, on_device(): lax.all_gather(grad_dot, 'seq', axis=0, tiled=True)  47.4 us
    dot_general x32, matrix products, tile(): jnp.einsum('qhd,khd->qhk', q_tile, k_heads, preferred_element_type=jnp.fl...  43.6 us
    dot_general x32, matrix products, tile(): jnp.einsum('qhk,qhd->khd', tile_probs.astype(jnp.bfloat16), g_tile, prefe...  37.8 us
  transfers between devices with their start and end apart: 4, of which 3 were waited for; matrix products, arithmetic and copies ran while one was open for 4% of the time, Pallas kernels for 0%

commit v1 on v0

--- a/solution.py
+++ b/solution.py
@@ -109,8 +109,11 @@
     k_heads = k_rows.reshape(row_count, heads_here, head_dim)
     v_heads = v_rows.reshape(row_count, heads_here, head_dim)
     zero_heads = jnp.zeros((row_count, heads_here, head_dim), jnp.float32)
-    q_piece = lax.all_gather(q_rows, "seq", axis=0, tiled=True)
-    g_piece = lax.all_gather(g_rows, "seq", axis=0, tiled=True)
+    q_piece, g_piece = jnp.split(
+        lax.all_gather(jnp.concatenate([q_rows, g_rows], axis=1), "seq", axis=0, tiled=True),
+        [q_rows.shape[1]],
+        axis=1,
+    )
     piece_rows = q_piece.shape[0]
     tile_rows = math.gcd(piece_rows, tile_limit)
 

time: 498 us -> 449 us (0.902)
  waiting for transfers between devices: 185 us -> 133 us
  blocking collectives: 132 us -> 123 us
  local copies, waits for them, and re-layouts: 11.9 us -> 17.6 us
    all_gather x2 -> x1, waiting for transfers between devices: 55.2 us -> 0.01 us  [on_device(): lax.all_gather(jnp.concatenate([q_rows, g_rows], axis=1), 'seq', axis=0,...]
    all_to_all x1 -> x0, blocking collectives: 9.16 us -> none  [on_device(): lax.all_to_all(out_grad, 'head', split_axis=1, concat_axis=0, tiled=True)]
    split x0 -> x1, local copies, waits for them, and re-layouts: none -> 5.74 us  [on_device(): jnp.split(lax.all_gather(jnp.concatenate([q_rows, g_rows], axis=1), 'seq'...]
where the time goes in v1:
time: 449 us; the launch traced here: 447 us
  matrix products  148 us (33%)
  waiting for transfers between devices  133 us (30%)
  blocking collectives  123 us (27%)
  local copies, waits for them, and re-layouts  17.6 us (4%)
  between operations  13.9 us (3%)
  starting transfers between devices  4.82 us (1%)
    all_gather x1, waiting for transfers between devices, on_device(): lax.all_gather(v_rows, 'seq', axis=0, tiled=True)  78.2 us
    all_gather x1, waiting for transfers between devices, on_device(): lax.all_gather(k_rows, 'seq', axis=0, tiled=True)  51.5 us
    all_gather x1, blocking collectives, on_device(): lax.all_gather(grad_dot, 'seq', axis=0, tiled=True)  48.3 us
    dot_general x32, matrix products, tile(): jnp.einsum('qhk,qhd->khd', tile_ds, q_tile, preferred_element_type=jnp.fl...  47.7 us
    all_gather x1, blocking collectives, on_device(): lax.all_gather(log_total, 'seq', axis=0, tiled=True)  47.6 us
    dot_general x32, matrix products, tile(): jnp.einsum('qhd,khd->qhk', q_tile, k_heads, preferred_element_type=jnp.fl...  43.6 us
    dot_general x32, matrix products, tile(): jnp.einsum('qhk,qhd->khd', tile_probs.astype(jnp.bfloat16), g_tile, prefe...  37.8 us
    dot_general x32, matrix products, tile(): allowed = jnp.einsum('qb,bk->qk', query_hot, key_table) > 0.5  11.2 us
  transfers between devices with their start and end apart: 4, of which 3 were waited for; matrix products, arithmetic and copies ran while one was open for 4% of the time, Pallas kernels for 0%

profile of v1, /device:TPU:8, one launch (start us, length us, event | category | flops | bytes accessed | tf_op | source)
XLA Modules:
  0.0 447.0 jit_solution(11789927174313754574)
XLA Ops:
  8.1 9.9 %all_to_all.76 = bf16[64,8,128]{2,0,1:T(8,128)(2,1)} all-to-all(bf16[64,8,128]{2,0,1:T(8,128)(2,1)S(1)} %copy_bitcast_fusion.2), channel_id=1, replica_groups=mesh['seq'=32,'head'=8] {'head'}, dimensions={1} | all-to-all | bytes 262144 | tf_op jit(solution)/shard_map/all_to_all | solution.py:32
  19.0 9.2 %all_to_all.77 = bf16[64,8,128]{2,0,1:T(8,128)(2,1)} all-to-all(bf16[64,8,128]{2,0,1:T(8,128)(2,1)S(1)} %copy_bitcast_fusion.3), channel_id=1, replica_groups=mesh['seq'=32,'head'=8] {'head'}, dimensions={1} | all-to-all | bytes 262144 | tf_op jit(solution)/shard_map/all_to_all | solution.py:33
  28.2 1.6 copy_bitcast_fusion
  29.7 4.7 %all-to-all-start.3 = ((bf16[64,8,128]{2,0,1:T(8,128)(2,1)}), bf16[64,8,128]{2,0,1:T(8,128)(2,1)S(1)}, u32[]{:S(2)}, u32[]{:S(2)}) async-start(bf16[64,8,128]{2,0,1:T(8,128)(2,1)} %copy_bitcast_fusion), calls=%async_computation.3 | async-start | bytes 262144 | tf_op jit(solution)/shard_map/all_to_all | solution.py:34
  35.4 3.7 all-to-all-done.3
  39.2 8.5 %all_to_all.78 = bf16[64,8,128]{2,0,1:T(8,128)(2,1)S(1)} all-to-all(bf16[64,8,128]{2,0,1:T(8,128)(2,1)S(1)} %copy_bitcast_fusion.1), channel_id=1, replica_groups=mesh['seq'=32,'head'=8] {'head'}, dimensions={1} | all-to-all | bytes 262144 | tf_op jit(solution)/shard_map/all_to_all | solution.py:31
  49.9 51.5 %all-gather.6.cloned.1.call-done = bf16[16384,128]{1,0:T(8,128)(2,1)} async-done(((bf16[512,128]{1,0:T(8,128)(2,1)}), bf16[16384,128]{1,0:T(8,128)(2,1)}) %all-gather.6.cloned.1.call-update) | async-done | bytes 4194320 | tf_op jit(solution)/shard_map/all_gather | solution.py:72
  101.4 2.9 gather_fusion.1
  104.3 78.2 %all-gather.4.cloned.1.call-done = bf16[16384,128]{1,0:T(8,128)(2,1)} async-done(((bf16[512,128]{1,0:T(8,128)(2,1)}), bf16[16384,128]{1,0:T(8,128)(2,1)}) %all-gather.4.cloned.1.call-update) | async-done | bytes 4194320 | tf_op jit(solution)/shard_map/all_gather | solution.py:73
  182.5 2.9 gather_fusion
  187.9 47.6 %all_gather.20 = f32[16384,1]{0,1:T(1,128)S(1)} all-gather(f32[512,1]{0,1:T(1,128)S(1)} %bitcast.245), channel_id=1, replica_groups=mesh['seq'=32,'head'=8] {'seq'}, dimensions={0}, use_global_device_ids=true | all-gather | bytes 67584 | tf_op jit(solution)/shard_map/all_gather | solution.py:103
  235.5 2.7 fusion.54
  238.2 48.3 %all_gather.21 = f32[16384,1]{0,1:T(1,128)S(1)} all-gather(f32[512,1]{0,1:T(1,128)S(1)} %bitcast.246), channel_id=1, replica_groups=mesh['seq'=32,'head'=8] {'seq'}, dimensions={0}, use_global_device_ids=true | all-gather | bytes 67584 | tf_op jit(solution)/shard_map/all_gather | solution.py:104
  286.4 3.4 fusion.41
  289.8 5.7 %fusion.63 = (bf16[16384,128]{1,0:T(8,128)(2,1)}, bf16[16384,128]{1,0:T(8,128)(2,1)}) fusion(bf16[16384,256]{1,0:T(8,128)(2,1)} %all-gather.8.cloned.1.call-done), kind=kLoop, calls=%fused_computation.107 | loop fusion | bytes 16777216 | tf_op jit(solution)/shard_map/split | solution.py:112
  295.6 143.3 %while.18 = (s32[]{:T(128)}, f32[512,1,128]{0,2,1:T(8,128)S(1)}, f32[512,1,128]{0,2,1:T(8,128)S(1)}, bf16[16384,128]{1,0:T(8,128)(2,1)}, bf16[128,512]{1,0:T(8,1...) while((s32[]{:T(128)}, f32[512,1,128]{0,2,1:T(8,128)S(1)}, ...), condition=%wide.region_5.7_spmd.clone, body=%wide.region_4.6_spmd.clone.sunk | while | flops 338239488 | bytes 5654229 | solution.py:153
  296.0 1.4 fusion.97
  297.4 1.5 fusion.98
  300.5 1.4 fusion.97
  301.9 1.5 fusion.98
  305.0 1.4 fusion.97
  306.3 1.5 fusion.98
  309.4 1.4 fusion.97
  310.8 1.5 fusion.98
  313.9 1.4 fusion.97
  315.3 1.5 fusion.98
  318.4 1.4 fusion.97
  319.8 1.5 fusion.98
  322.9 1.4 fusion.97
  324.2 1.5 fusion.98
  327.4 1.4 fusion.97
  328.7 1.5 fusion.98
  331.8 1.4 fusion.97
  333.2 1.5 fusion.98
  337.7 1.5 fusion.98
  342.2 1.5 fusion.98
  345.3 1.4 fusion.97
  346.6 1.5 fusion.98
  351.1 1.5 fusion.98
  355.6 1.5 fusion.98
  358.7 1.4 fusion.97
  360.1 1.5 fusion.98
  364.5 1.5 fusion.98
  369.0 1.5 fusion.98
  372.1 1.4 fusion.97
  373.5 1.5 fusion.98
  378.0 1.5 fusion.98
  382.5 1.5 fusion.98
  385.6 1.4 fusion.97
  386.9 1.5 fusion.98
  391.4 1.5 fusion.98
  395.9 1.5 fusion.98
  399.0 1.4 fusion.97
  400.4 1.5 fusion.98
  404.8 1.5 fusion.98
  409.3 1.5 fusion.98
  412.4 1.4 fusion.97
  413.8 1.5 fusion.98
  418.3 1.5 fusion.98
  422.7 1.5 fusion.98
  425.9 1.4 fusion.97
  427.2 1.5 fusion.98
  431.7 1.5 fusion.98
  436.2 1.5 fusion.98
  (192 shorter events, 80.4 us)
Async XLA Ops:
  7.2 0.9 copy-start
  7.2 41.2 %copy-start.5 = (s32[128,8]{0,1:T(8,128)S(1)}, s32[128,8]{0,1:T(8,128)}, u32[]{:S(2)}) copy-start(s32[128,8]{0,1:T(8,128)} %param.14) | copy-start | bytes 12292
  7.2 41.7 %copy-start.6 = (s32[128]{0:T(128)S(1)}, s32[128]{0:T(128)}, u32[]{:S(2)}) copy-start(s32[128]{0:T(128)} %param.15) | copy-start | bytes 1540
  7.2 94.2 %all-gather.6.cloned.1.call-start = ((), (), s32[]{:S(2)}) async-start(), calls=%async_computation.5 | async-start | bytes 4325376 | tf_op jit(solution)/shard_map/all_gather | solution.py:72
  18.0 164.5 %all-gather.4.cloned.1.call-start = ((), (), s32[]{:S(2)}) async-start(), calls=%async_computation.4 | async-start | bytes 4325376 | tf_op jit(solution)/shard_map/all_gather | solution.py:73
  29.7 9.4 %all-to-all-start.3 = ((bf16[64,8,128]{2,0,1:T(8,128)(2,1)}), bf16[64,8,128]{2,0,1:T(8,128)(2,1)S(1)}, u32[]{:S(2)}, u32[]{:S(2)}) async-start(bf16[64,8,128]{2,0,1:T(8,128)(2,1)} %copy_bitcast_fusion), calls=%async_computation.3 | async-start | bytes 262144 | tf_op jit(solution)/shard_map/all_to_all | solution.py:34
  34.5 255.4 %all-gather.8.cloned.1.call-start = ((), (), s32[]{:S(2)}) async-start(), calls=%async_computation.6 | async-start | bytes 8650752 | tf_op jit(solution)/shard_map/all_gather | solution.py:113
  185.7 2.1 copy-start.2
  185.7 49.7 %copy-start.3 = (bf16[4,8,128,1,128]{4,2,1,0,3:T(8,128)(2,1)}, bf16[4,8,128,1,128]{4,2,1,0,3:T(8,128)(2,1)S(1)}, u32[]{:S(2)}) copy-start(bf16[4,8,128,1,128]{4,2,1,0,3:T(8,128)(2,1)S(1)} %get-tuple-element.311) | copy-start | bytes 3145732
  289.8 5.8 %copy-start.1 = (bf16[64,8,128]{2,0,1:T(8,128)(2,1)S(1)}, bf16[64,8,128]{2,0,1:T(8,128)(2,1)}, u32[]{:S(2)}) copy-start(bf16[64,8,128]{2,0,1:T(8,128)(2,1)} %all_to_all.77) | copy-start | bytes 393220
  289.8 5.8 %copy-start.4 = (bf16[64,8,128]{2,0,1:T(8,128)(2,1)S(1)}, bf16[64,8,128]{2,0,1:T(8,128)(2,1)}, u32[]{:S(2)}) copy-start(bf16[64,8,128]{2,0,1:T(8,128)(2,1)} %all_to_all.76) | copy-start | bytes 393220
Sparse Core Ops, SparseCore 0:
  18.1 83.2 all-gather.5
  103.9 78.5 all-gather.3
  185.1 94.9 all-gather.7
